TPU v7x, 512 devices: a whole 4x8x8 slice. The times are simulated.
512 devices in a mesh: mode: 2 (over core), oth: 256 (over z, y, x).
Axes of the slice: x: 4, y: 8, z: 8, core: 2. Of those that a mesh axis runs over, the one named last changes fastest.
Arguments:
- tensor: float32 [512, 4, 262144], P('mode', None, 'oth'), may hold values from -20 to 20
- start_basis: float32 [512, 128], replicated, may hold values from -6 to 6
Outputs:
- core_slab: float32 [128, 4, 262144], P('mode', None, 'oth')
- triangle: float32 [512, 512], replicated
All inputs are finite; a program needn't handle non-finite values.
Results may differ from a plain program's by a relative error of at most 0.0003.
Values sent between devices are 32-bit elements; how exact they have to be, the bound alone decides.
A program may use at most 64 MiB of HBM per device.

v0:
```python
import jax
import jax.numpy as jnp
from jax import lax
from jax.sharding import PartitionSpec as P

ITERS = 3


def subspace(triangle, start_basis):
    basis = start_basis
    for sweep in range(ITERS):
        reduced = jnp.dot(
            triangle.T, basis, precision=lax.Precision.HIGHEST, preferred_element_type=jnp.float32
        )
        images = jnp.dot(
            triangle, reduced, precision=lax.Precision.HIGHEST, preferred_element_type=jnp.float32
        )
        gram_small = jnp.dot(
            images.T, images, precision=lax.Precision.HIGHEST, preferred_element_type=jnp.float32
        )
        factor_lower = jnp.linalg.cholesky(gram_small)
        basis = lax.linalg.triangular_solve(
            factor_lower, images, left_side=False, lower=True, transpose_a=True
        )
    return basis


def local(tensor, start_basis):
    rows_local, components, cell_count = tensor.shape
    group_size = lax.axis_size("mode")
    column_total = components * cell_count * lax.axis_size("oth")
    fibers_full = lax.all_to_all(tensor, "mode", split_axis=2, concat_axis=0, tiled=True)
    full_rows = fibers_full.shape[0]
    unfolded = fibers_full.reshape(full_rows, -1)
    covar_part = (
        jnp.dot(
            unfolded,
            unfolded.T,
            precision=lax.Precision.HIGHEST,
            preferred_element_type=jnp.float32,
        )
        / column_total
    )
    flat_part = covar_part.reshape(full_rows * full_rows)
    summed_piece = lax.psum_scatter(flat_part, ("mode", "oth"), scatter_dimension=0, tiled=True)
    summed_covar = lax.all_gather(summed_piece, ("mode", "oth"), axis=0, tiled=True).reshape(
        full_rows, full_rows
    )
    triangle = jnp.linalg.cholesky(summed_covar)
    basis = subspace(triangle, start_basis)
    rank_total = basis.shape[1]
    mode_index = lax.axis_index("mode")
    own_rows = lax.dynamic_slice_in_dim(basis, mode_index * rows_local, rows_local, 0)
    local_unfolded = tensor.reshape(rows_local, -1)
    product = lax.dot_general(
        own_rows,
        local_unfolded,
        (((0,), (0,)), ((), ())),
        precision=lax.Precision.HIGHEST,
        preferred_element_type=jnp.float32,
    )
    core_slab = lax.psum_scatter(
        product.reshape(lax.axis_size("mode") * (rank_total // group_size), components, cell_count),
        "mode",
        scatter_dimension=0,
        tiled=True,
    )
    return (core_slab, triangle)


def solution(mesh):
    return jax.shard_map(
        local,
        mesh=mesh,
        in_specs=(P("mode", None, "oth"), P()),
        out_specs=(P("mode", None, "oth"), P()),
        check_vma=False,
    )
```

profile of v0, /device:TPU:1, one launch (start us, length us, event | category | flops | bytes accessed | tf_op | source)
XLA Modules:
  0.0 643.0 jit_solution(9546581247558276727)
XLA Ops:
  7.2 0.0 all-reduce.4.cloned.1.call-start
  7.2 6.5 %copy.27 = f32[256,4,1024]{0,1,2:T(4,128)} copy(f32[256,4,1024]{2,1,0:T(4,128)} %param.5) | data formatting | bytes 8388608 | tf_op args[0]
  13.8 18.3 %all_to_all.15 = f32[256,4,1024]{0,1,2:T(4,128)} all-to-all(f32[256,4,1024]{0,1,2:T(4,128)} %copy.27), channel_id=1, replica_groups=mesh['mode'=2,'oth'=256] {'mode'}, dimensions={2} | all-to-all | bytes 8388608 | tf_op jit(solution)/shard_map/all_to_all | solution.py:32
  32.1 7.3 %copy.28 = f32[256,4,2,512]{3,1,0,2:T(4,128)} copy(f32[256,4,2,512]{0,1,3,2:T(4,128)} %bitcast.103) | data formatting | bytes 8388608 | tf_op jit(solution)/shard_map/all_to_all | solution.py:32
  39.4 4.1 copy.37
  43.5 6.9 %fusion = f32[64,4,8,128]{3,2,1,0:T(8,128)S(1)} fusion(f32[512,2048]{1,0:T(8,128)S(1)} %bitcast.100), kind=kOutput, calls=%fused_computation.1 | convolution fusion | flops 6442713088 | bytes 5242880 | tf_op jit(solution)/shard_map/dot_general | solution.py:36
  50.4 1.2 copy.38
  51.7 0.0 all-gather.3.cloned.1.call-start
  51.8 274.5 %all-reduce.4.cloned.1.call-done = f32[262144]{0:T(1024)} async-done(((f32[262144]{0:T(1024)}), f32[262144]{0:T(1024)}) %all-reduce.4.cloned.1.call-update) | async-done | bytes 1048592
  326.3 1.3 dynamic-slice
  327.7 11.7 %reduce-scatter.2.cloned.1.call-start = ((), (), s32[]{:S(2)}) async-start(), calls=%async_computation.2 | async-start | bytes 3145728 | tf_op jit(solution)/shard_map/reduce_scatter | solution.py:62
  339.4 8.0 %copy.39 = f32[32,8,4,1024]{3,1,2,0:T(8,128)} copy(f32[32,8,4,1024]{3,2,1,0:T(4,128)} %bitcast.101) | data formatting | bytes 8388608
  347.3 5.6 copy.34
  352.9 86.7 %all-gather.3.cloned.1.call-done = f32[512,1,512]{2,1,0:T(1,128)} async-done(((f32[1,1,512]{2,1,0:T(1,128)}), f32[512,1,512]{2,1,0:T(1,128)}) %all-gather.3.cloned.1.call-update) | async-done | bytes 1048592 | tf_op jit(solution)/shard_map/all_gather | solution.py:46
  439.6 2.3 copy.29
  442.0 1.4 fusion.1
  443.4 11.7 %cholesky.120 = f32[128,128]{1,0:T(8,128)S(1)} custom-call(f32[128,128]{1,0:T(8,128)S(1)} %cholesky.356), custom_call_target="Cholesky" | custom-call | tf_op jit(solution)/shard_map/jit(cholesky)/cholesky | solution.py:49
  455.2 9.8 %custom-call.32 = f32[1,128,128]{1,2,0:T(8,128)S(1)} custom-call(f32[1,128,128]{2,1,0:T(8,128)S(1)} %get-tuple-element.21), custom_call_target="InvertDiagBlocksLowerTriangular" | custom-call | tf_op jit(solution)/shard_map/jit(cholesky)/cholesky | solution.py:49
  465.0 0.1 cholesky.251
  465.1 0.3 constant_dynamic-update-slice_fusion.1
  465.4 0.3 convolution_subtract_fusion
  465.8 11.7 %cholesky.244 = f32[128,128]{1,0:T(8,128)S(1)} custom-call(f32[128,128]{1,0:T(8,128)S(1)} %cholesky.360), custom_call_target="Cholesky" | custom-call | tf_op jit(solution)/shard_map/jit(cholesky)/cholesky | solution.py:49
  477.5 10.2 %custom-call.33 = f32[1,128,128]{1,2,0:T(8,128)S(1)} custom-call(f32[1,128,128]{2,1,0:T(8,128)S(1)} %get-tuple-element.18), custom_call_target="InvertDiagBlocksLowerTriangular" | custom-call | tf_op jit(solution)/shard_map/jit(cholesky)/cholesky | solution.py:49
  487.7 0.3 convolution_dynamic-update-slice_fusion
  488.0 0.4 convolution_subtract_fusion.1
  488.4 11.7 %cholesky.265 = f32[128,128]{1,0:T(8,128)S(1)} custom-call(f32[128,128]{1,0:T(8,128)S(1)} %cholesky.365), custom_call_target="Cholesky" | custom-call | tf_op jit(solution)/shard_map/jit(cholesky)/cholesky | solution.py:49
  500.2 0.7 compare_reduce_fusion.4
  500.8 9.8 %custom-call.34 = f32[1,128,128]{1,2,0:T(8,128)S(1)} custom-call(f32[1,128,128]{2,1,0:T(8,128)S(1)} %get-tuple-element.15), custom_call_target="InvertDiagBlocksLowerTriangular" | custom-call | tf_op jit(solution)/shard_map/jit(cholesky)/cholesky | solution.py:49
  510.6 0.2 convolution_dynamic-update-slice_fusion.1
  510.8 0.4 convolution_subtract_fusion.2
  511.2 11.7 %cholesky.282 = f32[128,128]{1,0:T(8,128)S(1)} custom-call(f32[128,128]{1,0:T(8,128)S(1)} %convolution_subtract_fusion.2), custom_call_target="Cholesky" | custom-call | tf_op jit(solution)/shard_map/jit(cholesky)/cholesky | solution.py:49
  523.0 0.7 compare_reduce_fusion.3
  523.6 0.6 compare_reduce_fusion.5
  526.8 0.1 select_select_fusion
  527.0 2.0 fusion.44
  528.9 1.0 fusion.45
  529.9 0.6 fusion.46
  530.5 0.1 copy.31
  530.6 11.7 %cholesky.325 = f32[128,128]{1,0:T(8,128)S(1)} custom-call(f32[128,128]{1,0:T(8,128)S(1)} %fusion.21), custom_call_target="Cholesky" | custom-call | tf_op jit(solution)/shard_map/jit(cholesky)/cholesky | solution.py:21
  542.4 0.6 compare_reduce_fusion.2
  543.0 0.7 fusion.11
  543.7 9.8 %custom-call.37 = f32[1,128,128]{1,2,0:T(8,128)S(1)} custom-call(f32[1,128,128]{2,1,0:T(8,128)S(1)} %fusion.11), custom_call_target="InvertDiagBlocksLowerTriangular" | custom-call | tf_op jit(solution)/shard_map/triangular_solve/custom-call.8 | solution.py:22
  553.5 0.4 convolution_bitcast_fusion.2
  553.9 1.8 fusion.47
  555.7 1.2 fusion.48
  557.0 0.6 fusion.49
  557.5 0.1 copy.32
  557.7 11.7 %cholesky.336 = f32[128,128]{1,0:T(8,128)S(1)} custom-call(f32[128,128]{1,0:T(8,128)S(1)} %fusion.19), custom_call_target="Cholesky" | custom-call | tf_op jit(solution)/shard_map/jit(cholesky)/cholesky | solution.py:21
  569.4 0.6 compare_reduce_fusion.1
  570.1 0.7 fusion.12
  570.7 9.8 %custom-call.38 = f32[1,128,128]{1,2,0:T(8,128)S(1)} custom-call(f32[1,128,128]{2,1,0:T(8,128)S(1)} %fusion.12), custom_call_target="InvertDiagBlocksLowerTriangular" | custom-call | tf_op jit(solution)/shard_map/triangular_solve/custom-call.8 | solution.py:22
  580.5 0.4 convolution_bitcast_fusion.1
  581.0 1.8 fusion.50
  582.8 1.0 fusion.51
  583.8 0.6 fusion.52
  584.4 0.1 copy.33
  584.5 12.0 %cholesky.347 = f32[128,128]{1,0:T(8,128)S(1)} custom-call(f32[128,128]{1,0:T(8,128)S(1)} %fusion.17), custom_call_target="Cholesky" | custom-call | tf_op jit(solution)/shard_map/jit(cholesky)/cholesky | solution.py:21
  596.5 0.6 compare_reduce_fusion
  597.1 0.7 fusion.13
  597.8 9.8 %custom-call.39 = f32[1,128,128]{1,2,0:T(8,128)S(1)} custom-call(f32[1,128,128]{2,1,0:T(8,128)S(1)} %fusion.13), custom_call_target="InvertDiagBlocksLowerTriangular" | custom-call | tf_op jit(solution)/shard_map/triangular_solve/custom-call.8 | solution.py:22
  607.6 0.4 convolution_bitcast_fusion
  608.0 7.8 %fusion.8 = f32[128,4,1024]{2,0,1:T(8,128)} fusion(f32[4,1024,256]{2,1,0:T(8,128)} %bitcast.102, f32[512,128]{0,1:T(8,128)S(1)} %convolution_bitcast_fusion, s32[]{:T(128)S(6)} %select_n.11), kind=kOutput, calls=%fused_computation.20 | convolution fusion | flops 1610612736 | bytes 6422532 | tf_op jit(solution)/shard_map/dot_general | solution.py:55
  615.8 17.3 %reduce-scatter.2.cloned.1.call-done = f32[64,4,1024]{2,0,1:T(8,128)} async-done(((f32[128,4,1024]{2,0,1:T(8,128)}), f32[64,4,1024]{2,0,1:T(8,128)}) %reduce-scatter.2.cloned.1.call-update) | async-done | bytes 1048592 | tf_op jit(solution)/shard_map/reduce_scatter | solution.py:62
  633.1 2.9 copy.35
  (20 shorter events, 0.4 us)
Async XLA Ops:
  7.2 519.8 %copy-start = (f32[512,128]{1,0:T(8,128)S(1)}, f32[512,128]{1,0:T(8,128)}, u32[]{:S(2)}) copy-start(f32[512,128]{1,0:T(8,128)} %param.6) | copy-start | bytes 786436
  7.2 319.1 %all-reduce.4.cloned.1.call-start = ((), (), s32[]{:S(2)}) async-start(), calls=%async_computation.4 | async-start | bytes 2097152
  51.7 387.9 %all-gather.3.cloned.1.call-start = ((), (), s32[]{:S(2)}) async-start(), calls=%async_computation.3 | async-start | bytes 1050624 | tf_op jit(solution)/shard_map/all_gather | solution.py:46
  327.7 305.5 %reduce-scatter.2.cloned.1.call-start = ((), (), s32[]{:S(2)}) async-start(), calls=%async_computation.2 | async-start | bytes 3145728 | tf_op jit(solution)/shard_map/reduce_scatter | solution.py:62
  526.9 55.8 %copy-start.1 = (f32[512,512]{1,0:T(8,128)}, f32[512,512]{1,0:T(8,128)S(1)}, u32[]{:S(2)}) copy-start(f32[512,512]{1,0:T(8,128)S(1)} %select_select_fusion) | copy-start | bytes 3145732
Sparse Core Ops, SparseCore 0:
  51.8 274.4 all-reduce.3
  331.1 108.5 all-gather.2
  616.0 17.1 reduce-scatter.1
where the time goes:
time: 651 us; the launch traced here: 643 us
  waiting for transfers between devices  379 us (58%)
  other arithmetic  149 us (23%)
  local copies, waits for them, and re-layouts  39.7 us (6%)
  matrix products  28.3 us (4%)
  blocking collectives  18.3 us (3%)
  between operations  17 us (3%)
  starting transfers between devices  11.8 us (2%)
    unnamed x4, waiting for transfers between devices  275 us
    all_gather x1, waiting for transfers between devices, local(): lax.all_gather(summed_piece, ('mode', 'oth'), axis=0, tiled=True)  86.7 us
    another operation x14, other arithmetic, local(): triangle = jnp.linalg.cholesky(summed_covar)  78.8 us
    another operation x9, other arithmetic, subspace(): factor_lower = jnp.linalg.cholesky(gram_small)  37.4 us
    another operation x6, other arithmetic, subspace(): lax.linalg.triangular_solve(factor_lower, images, left_side=False, lower=...  31.4 us
    unnamed x10, local copies, waits for them, and re-layouts  24.1 us
    all_to_all x1, blocking collectives, local(): lax.all_to_all(tensor, 'mode', split_axis=2, concat_axis=0, tiled=True)  18.3 us
    reduce_scatter x1, waiting for transfers between devices, local(): lax.psum_scatter(product.reshape(lax.axis_size('mode') * (rank_total // g...  17.3 us
  transfers between devices with their start and end apart: 3, of which 3 were waited for; matrix products, arithmetic and copies ran while one was open for 2% of the time, Pallas kernels for 0%

commit v1 on v0

--- a/solution.py
+++ b/solution.py
@@ -43,9 +43,12 @@
     )
     flat_part = covar_part.reshape(full_rows * full_rows)
     summed_piece = lax.psum_scatter(flat_part, ("mode", "oth"), scatter_dimension=0, tiled=True)
-    summed_covar = lax.all_gather(summed_piece, ("mode", "oth"), axis=0, tiled=True).reshape(
-        full_rows, full_rows
-    )
+    summed_covar = jnp.concatenate(
+        lax.all_to_all(
+            jnp.stack([summed_piece] * lax.axis_size(("mode", "oth"))), ("mode", "oth"), 0, 0
+        ),
+        axis=0,
+    ).reshape(full_rows, full_rows)
     triangle = jnp.linalg.cholesky(summed_covar)
     basis = subspace(triangle, start_basis)
     rank_total = basis.shape[1]

time: 651 us -> 578 us (0.89)
  waiting for transfers between devices: 379 us -> 305 us
    all_gather x1 -> x0, waiting for transfers between devices: 86.7 us -> none  [local(): lax.all_gather(summed_piece, ('mode', 'oth'), axis=0, tiled=True)]
    all_to_all x0 -> x1, waiting for transfers between devices: none -> 18.7 us  [local(): lax.all_to_all(jnp.stack([summed_piece] * lax.axis_size(('mode', 'oth')))...]
    all_to_all x0 -> x1, starting transfers between devices: none -> 12.9 us  [local(): lax.all_to_all(jnp.stack([summed_piece] * lax.axis_size(('mode', 'oth')))...]
    reduce_scatter x1, starting transfers between devices: 11.7 us -> 0.04 us  [local(): lax.psum_scatter(product.reshape(lax.axis_size('mode') * (rank_total // g...]
    unnamed x4 -> x3, waiting for transfers between devices: 275 us -> 275 us
where the time goes in v1:
time: 578 us; the launch traced here: 569 us
  waiting for transfers between devices  305 us (53%)
  other arithmetic  148 us (26%)
  local copies, waits for them, and re-layouts  39.8 us (7%)
  matrix products  28.5 us (5%)
  blocking collectives  18.3 us (3%)
  between operations  17.1 us (3%)
  starting transfers between devices  13 us (2%)
    unnamed x3, waiting for transfers between devices  275 us
    another operation x14, other arithmetic, local(): triangle = jnp.linalg.cholesky(summed_covar)  78.6 us
    another operation x9, other arithmetic, subspace(): factor_lower = jnp.linalg.cholesky(gram_small)  37.4 us
    another operation x6, other arithmetic, subspace(): lax.linalg.triangular_solve(factor_lower, images, left_side=False, lower=...  31.4 us
    unnamed x10, local copies, waits for them, and re-layouts  23.5 us
    all_to_all x1, waiting for transfers between devices, local(): lax.all_to_all(jnp.stack([summed_piece] * lax.axis_size(('mode', 'oth')))...  18.7 us
    all_to_all x1, blocking collectives, local(): lax.all_to_all(tensor, 'mode', split_axis=2, concat_axis=0, tiled=True)  18.3 us
    all_to_all x1, starting transfers between devices, local(): lax.all_to_all(jnp.stack([summed_piece] * lax.axis_size(('mode', 'oth')))...  12.9 us
  transfers between devices with their start and end apart: 3, of which 3 were waited for; matrix products, arithmetic and copies ran while one was open for 2% of the time, Pallas kernels for 0%

profile of v1, /device:TPU:1, one launch (start us, length us, event | category | flops | bytes accessed | tf_op | source)
XLA Modules:
  0.0 569.5 jit_solution(8290222718828596842)
XLA Ops:
  7.2 6.5 %copy.26 = f32[256,4,1024]{0,1,2:T(4,128)} copy(f32[256,4,1024]{2,1,0:T(4,128)} %param.5) | data formatting | bytes 8388608 | tf_op args[0]
  13.8 18.3 %all_to_all.24 = f32[256,4,1024]{0,1,2:T(4,128)} all-to-all(f32[256,4,1024]{0,1,2:T(4,128)} %copy.26), channel_id=1, replica_groups=mesh['mode'=2,'oth'=256] {'mode'}, dimensions={2} | all-to-all | bytes 8388608 | tf_op jit(solution)/shard_map/all_to_all | solution.py:32
  32.1 7.3 %copy.27 = f32[256,4,2,512]{3,1,0,2:T(4,128)} copy(f32[256,4,2,512]{0,1,3,2:T(4,128)} %bitcast.102) | data formatting | bytes 8388608 | tf_op jit(solution)/shard_map/all_to_all | solution.py:32
  39.4 4.1 copy.36
  43.5 6.9 %fusion = f32[64,4,8,128]{3,2,1,0:T(8,128)S(1)} fusion(f32[512,2048]{1,0:T(8,128)S(1)} %bitcast.99), kind=kOutput, calls=%fused_computation.1 | convolution fusion | flops 6442713088 | bytes 5242880 | tf_op jit(solution)/shard_map/dot_general | solution.py:36
  50.4 1.2 copy.37
  51.7 274.6 %all-reduce.4.cloned.1.call-done = f32[262144]{0:T(1024)} async-done(((f32[262144]{0:T(1024)}), f32[262144]{0:T(1024)}) %all-reduce.4.cloned.1.call-update) | async-done | bytes 1048592
  326.3 0.8 dynamic-slice
  327.0 1.5 stack.2
  328.5 12.9 %all-to-all-start.1 = ((f32[512,1,512]{2,1,0:T(1,128)}), f32[512,1,512]{2,1,0:T(1,128)S(1)}, u32[]{:S(2)}, u32[]{:S(2)}) async-start(f32[512,1,512]{2,1,0:T(1,128)} %stack.2), calls=%async_computation.1 | async-start | bytes 2097152 | tf_op jit(solution)/shard_map/all_to_all | solution.py:47
  341.4 0.0 reduce-scatter.2.cloned.1.call-start
  341.5 8.0 %copy.38 = f32[32,8,4,1024]{3,1,2,0:T(8,128)} copy(f32[32,8,4,1024]{3,2,1,0:T(4,128)} %bitcast.100) | data formatting | bytes 8388608
  349.4 5.6 copy.33
  355.0 18.7 %all-to-all-done.1 = f32[512,1,512]{2,1,0:T(1,128)S(1)} async-done(((f32[512,1,512]{2,1,0:T(1,128)}), f32[512,1,512]{2,1,0:T(1,128)S(1)}, u32[]{:S(2)}, u32[]{:S(2)}) %all-to-all-start.1) | async-done | bytes 1048608 | tf_op jit(solution)/shard_map/all_to_all | solution.py:47
  373.8 1.5 copy.28
  375.2 0.2 fusion.1
  375.5 11.7 %cholesky.120 = f32[128,128]{1,0:T(8,128)S(1)} custom-call(f32[128,128]{1,0:T(8,128)S(1)} %cholesky.356), custom_call_target="Cholesky" | custom-call | tf_op jit(solution)/shard_map/jit(cholesky)/cholesky | solution.py:52
  387.2 9.8 %custom-call.32 = f32[1,128,128]{1,2,0:T(8,128)S(1)} custom-call(f32[1,128,128]{2,1,0:T(8,128)S(1)} %get-tuple-element.21), custom_call_target="InvertDiagBlocksLowerTriangular" | custom-call | tf_op jit(solution)/shard_map/jit(cholesky)/cholesky | solution.py:52
  397.1 0.1 cholesky.251
  397.2 0.3 constant_dynamic-update-slice_fusion.1
  397.5 0.3 convolution_subtract_fusion
  397.9 11.7 %cholesky.244 = f32[128,128]{1,0:T(8,128)S(1)} custom-call(f32[128,128]{1,0:T(8,128)S(1)} %cholesky.360), custom_call_target="Cholesky" | custom-call | tf_op jit(solution)/shard_map/jit(cholesky)/cholesky | solution.py:52
  409.6 10.0 %custom-call.33 = f32[1,128,128]{1,2,0:T(8,128)S(1)} custom-call(f32[1,128,128]{2,1,0:T(8,128)S(1)} %get-tuple-element.18), custom_call_target="InvertDiagBlocksLowerTriangular" | custom-call | tf_op jit(solution)/shard_map/jit(cholesky)/cholesky | solution.py:52
  419.6 0.3 convolution_dynamic-update-slice_fusion
  419.9 0.4 convolution_subtract_fusion.1
  420.3 11.7 %cholesky.265 = f32[128,128]{1,0:T(8,128)S(1)} custom-call(f32[128,128]{1,0:T(8,128)S(1)} %cholesky.365), custom_call_target="Cholesky" | custom-call | tf_op jit(solution)/shard_map/jit(cholesky)/cholesky | solution.py:52
  432.0 0.7 compare_reduce_fusion.4
  432.7 9.8 %custom-call.34 = f32[1,128,128]{1,2,0:T(8,128)S(1)} custom-call(f32[1,128,128]{2,1,0:T(8,128)S(1)} %get-tuple-element.15), custom_call_target="InvertDiagBlocksLowerTriangular" | custom-call | tf_op jit(solution)/shard_map/jit(cholesky)/cholesky | solution.py:52
  442.5 0.2 convolution_dynamic-update-slice_fusion.1
  442.7 0.4 convolution_subtract_fusion.2
  443.1 11.7 %cholesky.282 = f32[128,128]{1,0:T(8,128)S(1)} custom-call(f32[128,128]{1,0:T(8,128)S(1)} %convolution_subtract_fusion.2), custom_call_target="Cholesky" | custom-call | tf_op jit(solution)/shard_map/jit(cholesky)/cholesky | solution.py:52
  454.8 0.7 compare_reduce_fusion.3
  455.5 0.6 compare_reduce_fusion.5
  458.7 0.1 select_select_fusion
  458.8 2.2 fusion.44
  461.0 1.0 fusion.45
  462.0 0.6 fusion.46
  462.6 0.1 copy.30
  462.8 11.7 %cholesky.325 = f32[128,128]{1,0:T(8,128)S(1)} custom-call(f32[128,128]{1,0:T(8,128)S(1)} %fusion.21), custom_call_target="Cholesky" | custom-call | tf_op jit(solution)/shard_map/jit(cholesky)/cholesky | solution.py:21
  474.5 0.6 compare_reduce_fusion.2
  475.1 0.7 fusion.11
  475.8 9.8 %custom-call.37 = f32[1,128,128]{1,2,0:T(8,128)S(1)} custom-call(f32[1,128,128]{2,1,0:T(8,128)S(1)} %fusion.11), custom_call_target="InvertDiagBlocksLowerTriangular" | custom-call | tf_op jit(solution)/shard_map/triangular_solve/custom-call.8 | solution.py:22
  485.6 0.4 convolution_bitcast_fusion.2
  486.0 1.8 fusion.47
  487.9 1.2 fusion.48
  489.0 0.6 fusion.49
  489.6 0.1 copy.31
  489.7 11.7 %cholesky.336 = f32[128,128]{1,0:T(8,128)S(1)} custom-call(f32[128,128]{1,0:T(8,128)S(1)} %fusion.19), custom_call_target="Cholesky" | custom-call | tf_op jit(solution)/shard_map/jit(cholesky)/cholesky | solution.py:21
  501.5 0.6 compare_reduce_fusion.1
  502.1 0.7 fusion.12
  502.8 9.8 %custom-call.38 = f32[1,128,128]{1,2,0:T(8,128)S(1)} custom-call(f32[1,128,128]{2,1,0:T(8,128)S(1)} %fusion.12), custom_call_target="InvertDiagBlocksLowerTriangular" | custom-call | tf_op jit(solution)/shard_map/triangular_solve/custom-call.8 | solution.py:22
  512.6 0.4 convolution_bitcast_fusion.1
  513.0 1.8 fusion.50
  514.9 1.0 fusion.51
  515.8 0.6 fusion.52
  516.4 0.1 copy.32
  516.6 11.9 %cholesky.347 = f32[128,128]{1,0:T(8,128)S(1)} custom-call(f32[128,128]{1,0:T(8,128)S(1)} %fusion.17), custom_call_target="Cholesky" | custom-call | tf_op jit(solution)/shard_map/jit(cholesky)/cholesky | solution.py:21
  528.5 0.6 compare_reduce_fusion
  529.1 0.7 fusion.13
  529.8 9.8 %custom-call.39 = f32[1,128,128]{1,2,0:T(8,128)S(1)} custom-call(f32[1,128,128]{2,1,0:T(8,128)S(1)} %fusion.13), custom_call_target="InvertDiagBlocksLowerTriangular" | custom-call | tf_op jit(solution)/shard_map/triangular_solve/custom-call.8 | solution.py:22
  539.6 0.4 convolution_bitcast_fusion
  540.0 7.8 %fusion.8 = f32[128,4,1024]{2,0,1:T(8,128)} fusion(f32[4,1024,256]{2,1,0:T(8,128)} %bitcast.101, f32[512,128]{0,1:T(8,128)S(1)} %convolution_bitcast_fusion, s32[]{:T(128)S(6)} %select_n.11), kind=kOutput, calls=%fused_computation.20 | convolution fusion | flops 1610612736 | bytes 6422532 | tf_op jit(solution)/shard_map/dot_general | solution.py:58
  547.9 11.7 %reduce-scatter.2.cloned.1.call-done = f32[64,4,1024]{2,0,1:T(8,128)} async-done(((f32[128,4,1024]{2,0,1:T(8,128)}), f32[64,4,1024]{2,0,1:T(8,128)}) %reduce-scatter.2.cloned.1.call-update) | async-done | bytes 1048592 | tf_op jit(solution)/shard_map/reduce_scatter | solution.py:65
  559.5 2.9 copy.34
  (20 shorter events, 0.4 us)
Async XLA Ops:
  7.2 451.7 %copy-start = (f32[512,128]{1,0:T(8,128)S(1)}, f32[512,128]{1,0:T(8,128)}, u32[]{:S(2)}) copy-start(f32[512,128]{1,0:T(8,128)} %param.6) | copy-start | bytes 786436
  7.2 319.1 %all-reduce.4.cloned.1.call-start = ((), (), s32[]{:S(2)}) async-start(), calls=%async_computation.4 | async-start | bytes 2097152
  328.5 45.2 %all-to-all-start.1 = ((f32[512,1,512]{2,1,0:T(1,128)}), f32[512,1,512]{2,1,0:T(1,128)S(1)}, u32[]{:S(2)}, u32[]{:S(2)}) async-start(f32[512,1,512]{2,1,0:T(1,128)} %stack.2), calls=%async_computation.1 | async-start | bytes 2097152 | tf_op jit(solution)/shard_map/all_to_all | solution.py:47
  341.4 218.1 %reduce-scatter.2.cloned.1.call-start = ((), (), s32[]{:S(2)}) async-start(), calls=%async_computation.3 | async-start | bytes 3145728 | tf_op jit(solution)/shard_map/reduce_scatter | solution.py:65
  458.8 56.0 %copy-start.1 = (f32[512,512]{1,0:T(8,128)}, f32[512,512]{1,0:T(8,128)S(1)}, u32[]{:S(2)}) copy-start(f32[512,512]{1,0:T(8,128)S(1)} %select_select_fusion) | copy-start | bytes 3145732
Sparse Core Ops, SparseCore 0:
  51.8 274.4 all-reduce.3
  548.0 11.4 reduce-scatter.1
